TPU v7x, 256 devices: a whole 4x4x8 slice. The times are simulated.
256 devices in a mesh: song: 4 (over y), seq: 64 (over z, x, core).
Axes of the slice: x: 4, y: 4, z: 8, core: 2. Of those that a mesh axis runs over, the one named last changes fastest.
Arguments:
- queries: bfloat16 [4, 8192, 2048], P('song', 'seq'), may hold values from -64 to 64
- keys: bfloat16 [4, 8192, 2048], P('song', 'seq'), may hold values from -64 to 64
- values: bfloat16 [4, 8192, 2048], P('song', 'seq'), may hold values from -6 to 6
- lyric_keys: bfloat16 [4, 384, 2048], P('song', 'seq'), may hold values from -64 to 64
- lyric_values: bfloat16 [4, 384, 2048], P('song', 'seq'), may hold values from -6 to 6
- q_gain: float32 [128], replicated, may hold values from 0.5 to 1.5
- k_gain: float32 [128], replicated, may hold values from 0.5 to 1.5
- cotangent: bfloat16 [4, 8192, 2048], P('song', 'seq'), may hold values from -12 to 12
- alignment: int32 [4, 64, 2], P('song', 'seq'), may hold values from -1 to 2, as said below
- lyric_len: int32 [4], P('song'), may hold values from 192 to 384
Outputs:
- attn_out: bfloat16 [4, 8192, 2048], P('song', 'seq')
- grad_queries: bfloat16 [4, 8192, 2048], P('song', 'seq')
- grad_keys: bfloat16 [4, 8192, 2048], P('song', 'seq')
- grad_values: bfloat16 [4, 8192, 2048], P('song', 'seq')
- grad_lyric_keys: bfloat16 [4, 384, 2048], P('song', 'seq')
- grad_lyric_values: bfloat16 [4, 384, 2048], P('song', 'seq')
- grad_q_gain: float32 [128], replicated
- grad_k_gain: float32 [128], replicated
Inputs may be any that keep to these rules, and one draw needn't show every extreme that they name: `alignment`: in each row the entries that are not -1 are distinct.
All inputs are finite; a program needn't handle non-finite values.
Results may differ from a plain program's by a relative error of at most 0.01.
Values may be sent and summed in bfloat16 or wider, within the bound.
A program may use at most 128 MiB of HBM per device.

v0:
```python
import jax
import jax.numpy as jnp
from jax import lax
from jax.sharding import PartitionSpec as P

BLK = 128
WIN = 1
TILES = 2
NORM_EPS = 1e-06


def extended_2(block, sides, width):
    for axis, dim in sides:
        count = lax.axis_size(axis)
        forward = [(i, i + 1) for i in range(count - 1)]
        backward = [(target, source) for source, target in forward]
        low = lax.ppermute(
            lax.slice_in_dim(block, block.shape[dim] - width, None, axis=dim), axis, forward
        )
        high = lax.ppermute(lax.slice_in_dim(block, 0, width, axis=dim), axis, backward)
        block = jnp.concatenate([low, block, high], axis=dim)
    return block


def norm_heads(inputs, norm_gain):
    row_values = inputs.astype(jnp.float32).reshape(inputs.shape[0], -1, norm_gain.shape[0])
    inverse = lax.rsqrt(jnp.mean(row_values * row_values, axis=-1, keepdims=True) + NORM_EPS)
    return (row_values * inverse * norm_gain, inverse)


def norm_back(inputs, inverse, norm_gain, grad_out):
    row_values = inputs.astype(jnp.float32).reshape(grad_out.shape)
    scaled = grad_out * norm_gain
    grad_input = inverse * scaled - row_values * inverse * inverse * inverse * jnp.mean(
        scaled * row_values, axis=-1, keepdims=True
    )
    grad_gain = jnp.sum(grad_out * row_values * inverse, axis=(0, 1))
    return (grad_input.reshape(inputs.shape), grad_gain)


def block_pass(query_rows, key_rows, value_rows, keep_mask, grad_rows, score_scale):
    scores = (
        jnp.einsum("qhd,khd->hqk", query_rows, key_rows, preferred_element_type=jnp.float32)
        * score_scale
    )
    exp_scores = jnp.where(keep_mask[None, None, :], jnp.exp(scores), 0.0)
    totals = jnp.sum(exp_scores, axis=2)
    prob_full = exp_scores / totals[:, :, None]
    prob_low = prob_full.astype(jnp.bfloat16)
    block_output = jnp.einsum(
        "hqk,khd->qhd", prob_low, value_rows, preferred_element_type=jnp.float32
    ).astype(jnp.bfloat16)
    delta_rows = jnp.sum(grad_rows.astype(jnp.float32) * block_output.astype(jnp.float32), axis=2).T
    grad_prob = jnp.einsum(
        "qhd,khd->hqk", grad_rows, value_rows, preferred_element_type=jnp.float32
    )
    grad_score = (prob_full * (grad_prob - delta_rows[:, :, None])).astype(jnp.bfloat16)
    query_gradient = (
        jnp.einsum("hqk,khd->qhd", grad_score, key_rows, preferred_element_type=jnp.float32)
        * score_scale
    )
    grad_key = (
        jnp.einsum("hqk,qhd->khd", grad_score, query_rows, preferred_element_type=jnp.float32)
        * score_scale
    )
    value_gradient = jnp.einsum(
        "hqk,qhd->khd", prob_low, grad_rows, preferred_element_type=jnp.float32
    )
    return (block_output, query_gradient, grad_key, value_gradient, totals, delta_rows)


def body(
    queries, keys, values, lyric_keys, lyric_values, q_gain, k_gain, cotangent, alignment, lyric_len
):
    head_size = q_gain.shape[0]
    model_width = queries.shape[2]
    head_count = model_width // head_size
    frames = queries.shape[1]
    lyric_local = lyric_keys.shape[1]
    blocks = frames // BLK
    border_rows = WIN * BLK
    window_extent = (2 * WIN + 1) * BLK
    score_scale = head_size ** (-0.5)
    total_frames = frames * lax.axis_size("seq")
    first_frame = lax.axis_index("seq") * frames
    query_raw = queries[0]
    key_raw = keys[0]
    query_full, query_inv = norm_heads(query_raw, q_gain)
    key_full, key_inv = norm_heads(key_raw, k_gain)
    lyric_full, lyric_inv = norm_heads(lyric_keys[0], k_gain)
    query_norm = query_full.astype(jnp.bfloat16)
    key_norm = key_full.astype(jnp.bfloat16)
    lyric_norm = lyric_full.astype(jnp.bfloat16)
    lyric_key_all, lyric_val_all = (
        lax.all_gather(lyric_norm.reshape(lyric_local, model_width), "seq", axis=0, tiled=True),
        lax.all_gather(lyric_values[0], "seq", axis=0, tiled=True),
    )
    lyric_total = lyric_key_all.shape[0]
    lyric_key_all = lyric_key_all.reshape(lyric_total, head_count, head_size)
    lyric_val_all = lyric_val_all.reshape(lyric_total, head_count, head_size)
    stacked = jnp.stack([key_norm.reshape(frames, model_width), values[0]])
    extended = extended_2(stacked, (("seq", 1),), border_rows)
    ext_keys = extended[0].reshape(frames + 2 * border_rows, head_count, head_size)
    ext_vals = extended[1].reshape(frames + 2 * border_rows, head_count, head_size)
    grad_heads = cotangent[0].reshape(frames, head_count, head_size)
    length = lyric_len[0]

    def one_block(block_id):
        start_offset = block_id * BLK
        position = (
            first_frame + start_offset - border_rows + jnp.arange(window_extent, dtype=jnp.int32)
        )
        audio_mask = (position >= 0) & (position < total_frames)
        tile_ids = alignment[0, block_id]
        row_grid = (jnp.maximum(tile_ids, 0) * BLK)[:, None] + jnp.arange(BLK, dtype=jnp.int32)[
            None, :
        ]
        lyric_mask = ((tile_ids >= 0)[:, None] & (row_grid < length)).reshape(-1)
        row_index = row_grid.reshape(-1)
        all_keys = jnp.concatenate([ext_keys, jnp.take(lyric_key_all, row_index, axis=0)], axis=0)
        all_vals = jnp.concatenate([ext_vals, jnp.take(lyric_val_all, row_index, axis=0)], axis=0)
        keep_mask = jnp.concatenate([audio_mask, lyric_mask], axis=0)
        results = block_pass(query_norm, all_keys, all_vals, keep_mask, grad_heads, score_scale)
        return results + (row_index,)

    output_list, grad_qn, grad_key, value_gradient, totals, delta_rows, row_index = lax.map(
        one_block, jnp.arange(blocks, dtype=jnp.int32)
    )
    audio_cols = grad_key.shape[1] - TILES * BLK
    flat_rows = row_index.reshape(-1)
    lyric_grad_key = (
        jnp.zeros((lyric_total, head_count, head_size), jnp.float32)
        .at[flat_rows]
        .add(grad_key[:, audio_cols:].reshape(-1, head_count, head_size))
    )
    lyric_grad_val = (
        jnp.zeros((lyric_total, head_count, head_size), jnp.float32)
        .at[flat_rows]
        .add(value_gradient[:, audio_cols:].reshape(-1, head_count, head_size))
    )
    ext_grad_key = jnp.zeros((frames + 2 * border_rows, head_count, head_size), jnp.float32)
    ext_grad_val = jnp.zeros((frames + 2 * border_rows, head_count, head_size), jnp.float32)
    block_id = 0
    lower = block_id * BLK
    ext_grad_key = ext_grad_key.at[lower : lower + window_extent].add(
        grad_key[block_id, :window_extent]
    )
    ext_grad_val = ext_grad_val.at[lower : lower + window_extent].add(
        value_gradient[block_id, :window_extent]
    )
    own_grad_key = ext_grad_key[border_rows : border_rows + frames]
    own_grad_val = ext_grad_val[border_rows : border_rows + frames]
    rims = jnp.stack(
        [
            jnp.concatenate(
                [ext_grad_key[:border_rows], ext_grad_key[border_rows + frames :]], axis=0
            ).reshape(2 * border_rows, model_width),
            jnp.concatenate(
                [ext_grad_val[:border_rows], ext_grad_val[border_rows + frames :]], axis=0
            ).reshape(2 * border_rows, model_width),
        ]
    )
    received = extended_2(rims.astype(jnp.bfloat16), (("seq", 1),), border_rows).astype(rims.dtype)
    from_left = received[:, :border_rows].reshape(2, border_rows, head_count, head_size)
    from_right = received[:, 3 * border_rows :].reshape(2, border_rows, head_count, head_size)
    own_grad_key = (
        own_grad_key.at[:border_rows]
        .add(from_left[0])
        .at[frames - border_rows :]
        .add(from_right[0])
    )
    own_grad_val = (
        own_grad_val.at[:border_rows]
        .add(from_left[1])
        .at[frames - border_rows :]
        .add(from_right[1])
    )
    unnormed_query_gradient, query_gain_vector = norm_back(
        query_raw, query_inv, q_gain, grad_qn.reshape(frames, head_count, head_size)
    )
    unnormed_key_gradient, key_gain_vector = norm_back(key_raw, key_inv, k_gain, own_grad_key)
    summed_key, summed_val = (
        lax.psum_scatter(
            lyric_grad_key.reshape(lyric_total, model_width), "seq", scatter_dimension=0, tiled=True
        ),
        lax.psum_scatter(
            lyric_grad_val.reshape(lyric_total, model_width), "seq", scatter_dimension=0, tiled=True
        ),
    )
    unnormed_lyric_gradient, lyric_gain_vector = norm_back(
        lyric_keys[0], lyric_inv, k_gain, summed_key.reshape(lyric_local, head_count, head_size)
    )
    total_query_gain, total_key_gain = lax.psum(
        (query_gain_vector, key_gain_vector + lyric_gain_vector), ("song", "seq")
    )
    return (
        output_list.reshape(1, frames, model_width),
        unnormed_query_gradient.astype(jnp.bfloat16)[None],
        unnormed_key_gradient.astype(jnp.bfloat16)[None],
        own_grad_val.reshape(1, frames, model_width).astype(jnp.bfloat16),
        unnormed_lyric_gradient.astype(jnp.bfloat16)[None],
        summed_val.astype(jnp.bfloat16)[None],
        total_query_gain,
        total_key_gain,
    )


def solution(mesh):
    in_specs = (
        P("song", "seq", None),
        P("song", "seq", None),
        P("song", "seq", None),
        P("song", "seq", None),
        P("song", "seq", None),
        P(),
        P(),
        P("song", "seq", None),
        P("song", "seq", None),
        P("song"),
    )
    out_specs = (
        P("song", "seq", None),
        P("song", "seq", None),
        P("song", "seq", None),
        P("song", "seq", None),
        P("song", "seq", None),
        P("song", "seq", None),
        P(),
        P(),
    )
    return jax.shard_map(body, mesh=mesh, in_specs=in_specs, out_specs=out_specs, check_vma=False)
```

profile of v0, /device:TPU:1, one launch (start us, length us, event | category | flops | bytes accessed | tf_op | source)
XLA Modules:
  0.0 654.3 jit_solution(4677205366677550377)
XLA Ops:
  16.2 5.2 collective-permute-start.1
  27.9 5.7 collective-permute-done.1
  40.4 53.5 %all-gather.5.cloned.1.call-done = bf16[1,384,2048]{2,0,1:T(2,128)(2,1)} async-done(((bf16[1,6,2048]{2,0,1:T(2,128)(2,1)}), bf16[1,384,2048]{2,0,1:T(2,128)(2,1)}) %all-gather.5.cloned.1.call-update) | async-done | bytes 1572880 | tf_op jit(solution)/shard_map/all_gather | solution.py:96
  93.9 6.9 %copy.100 = bf16[1,384,2048]{1,2,0:T(8,128)(2,1)S(1)} copy(bf16[1,384,2048]{2,0,1:T(2,128)(2,1)} %all-gather.5.cloned.1.call-done) | data formatting | bytes 3145728 | tf_op jit(solution)/shard_map/all_gather | solution.py:96
  102.9 69.1 %all-gather.7.cloned.1.call-done = bf16[64,6,2048]{2,1,0:T(8,128)(2,1)} async-done(((bf16[1,6,2048]{2,1,0:T(8,128)(2,1)}), bf16[64,6,2048]{2,1,0:T(8,128)(2,1)}) %all-gather.7.cloned.1.call-update) | async-done | bytes 1572880 | tf_op jit(solution)/shard_map/all_gather | solution.py:95
  172.0 4.4 reshape.472
  176.4 3.2 gather_fusion.1
  186.3 3.1 fusion.56
  189.5 2.4 multiply_reduce_fusion
  196.8 2.1 fusion.55
  198.9 2.1 collective-permute-start.3
  201.0 3.6 collective-permute-start.2
  207.0 20.2 %scatter_fusion = f32[384,16,128]{2,1,0:T(8,128)S(1)} fusion(f32[384,16,128]{2,1,0:T(8,128)S(1)} %broadcast.403.clone, s32[256]{0:T(256)S(1)} %bitcast.227, f32[256,16,128]{2,1,0:T(8,128)} %copy.112), kind=kCustom, calls=%fused_computation.2 | custom fusion | flops 524288 | bytes 6292480 | tf_op jit(solution)/shard_map/scatter-add | solution.py:134
  227.3 3.1 copy.146
  234.4 20.2 %scatter_fusion.1 = f32[384,16,128]{2,1,0:T(8,128)S(1)} fusion(f32[384,16,128]{2,1,0:T(8,128)S(1)} %broadcast.403.clone.1, s32[256]{0:T(256)S(1)} %bitcast.228, f32[256,16,128]{2,1,0:T(8,128)} %copy.113), kind=kCustom, calls=%fused_computation.3 | custom fusion | flops 524288 | bytes 6292480 | tf_op jit(solution)/shard_map/scatter-add | solution.py:139
  254.6 3.1 copy.145
  257.7 279.7 %all-reduce.7 = bf16[384,2048]{1,0:T(8,128)(2,1)} all-reduce(f32[384,2048]{1,0:T(8,128)} %bitcast.203), channel_id=4, replica_groups=mesh['song'=4,'seq'=64] {'seq'}, use_global_device_ids=true, to_apply=%region_11.13.clone | all-reduce | flops 786432 | bytes 4718592
  537.4 4.1 fusion.18
  542.9 2.4 slice.228
  545.3 2.0 copy.114
  547.4 2.3 fusion.25
  549.7 2.0 copy.115
  557.9 2.0 copy.116
  565.4 82.4 %all-reduce.2 = (f32[128]{0:T(128)}, f32[128]{0:T(128)}) all-reduce(f32[128]{0:T(128)S(1)} %get-tuple-element.214, f32[128]{0:T(128)S(1)} %add.202), channel_id=1, replica_groups=mesh['song'=4,'seq'=64] {'song','seq'}, use_global_device_ids=true, to_apply=%region_13.15 | all-reduce | flops 256 | bytes 2048 | tf_op jit(solution)/shard_map/psum | solution.py:193
  (126 shorter events, 53.6 us)
Async XLA Ops:
  7.2 86.8 %all-gather.5.cloned.1.call-start = ((), (), s32[]{:S(2)}) async-start(), calls=%async_computation | async-start | bytes 3194880 | tf_op jit(solution)/shard_map/all_gather | solution.py:96
  8.7 163.3 %all-gather.7.cloned.1.call-start = ((), (), s32[]{:S(2)}) async-start(), calls=%async_computation.1 | async-start | bytes 2129920 | tf_op jit(solution)/shard_map/all_gather | solution.py:95
  11.7 550.9 %all-reduce.6.cloned.1.call-start = ((), (), s32[]{:S(2)}) async-start(), calls=%async_computation.2 | async-start | bytes 6291456
  13.1 10.9 %copy-start.24 = (s32[1,1,2]{2,1,0:T(1,128)S(1)}, s32[1,1,2]{2,1,0:T(1,128)}, u32[]{:S(2)}) copy-start(s32[1,1,2]{2,1,0:T(1,128)} %param.44) | copy-start | bytes 28
  13.1 11.0 %copy-start.19 = (bf16[1,128,2048]{2,1,0:T(8,128)(2,1)S(1)}, bf16[1,128,2048]{2,1,0:T(8,128)(2,1)}, u32[]{:S(2)}) copy-start(bf16[1,128,2048]{2,1,0:T(8,128)(2,1)} %param.43) | copy-start | bytes 1572868
  14.5 9.6 %copy-start.3 = (bf16[1,128,2048]{1,2,0:T(8,128)(2,1)}, bf16[1,128,2048]{1,2,0:T(8,128)(2,1)S(1)}, u32[]{:S(2)}) copy-start(bf16[1,128,2048]{1,2,0:T(8,128)(2,1)S(1)} %copy.97) | copy-start | bytes 1572868
  15.7 10.7 %copy-start.25 = (u32[256]{0:T(256)S(1)}, u32[256]{0:T(256)}, u32[]{:S(2)}) copy-start(u32[256]{0:T(256)} %constant.274) | copy-start | bytes 3076
  16.1 11.7 %copy-start.23 = (f32[128]{0:T(128)S(1)}, f32[128]{0:T(128)}, u32[]{:S(2)}) copy-start(f32[128]{0:T(128)} %param.41) | copy-start | bytes 1540
  16.2 17.4 %collective-permute-start.1 = (bf16[2,128,2048]{1,2,0:T(8,128)(2,1)S(1)}, bf16[2,128,2048]{1,2,0:T(8,128)(2,1)}, u32[]{:S(2)}, u32[]{:S(2)}) collective-permute-start(bf16[2,128,2048]{1,2,0:T(8,128)(2,1)S(1)} %pad_maximum_fusion.9), channel_id=1, source_target_pairs={{1,0},{2,1},{3,2},{4,3},{5,4},{6,5},{7,6},{8,7},{9,8},{10,9},{11,1... | collective-permute-start | bytes 3145736 | tf_op jit(solution)/shard_map/ppermute | solution.py:20
  21.4 14.2 %collective-permute-start = (bf16[2,128,2048]{1,2,0:T(8,128)(2,1)S(1)}, bf16[2,128,2048]{1,2,0:T(8,128)(2,1)}, u32[]{:S(2)}, u32[]{:S(2)}) collective-permute-start(bf16[2,128,2048]{1,2,0:T(8,128)(2,1)S(1)} %pad_maximum_fusion.9), channel_id=1, source_target_pairs={{0,1},{1,2},{2,3},{3,4},{4,5},{5,6},{6,7},{7,8},{8,9},{9,10},{10,1... | collective-permute-start | bytes 3145736 | tf_op jit(solution)/shard_map/ppermute | solution.py:17
  26.4 167.4 %copy-start.1 = (f32[1,128,2048]{1,2,0:T(8,128)}, f32[1,128,2048]{1,2,0:T(8,128)S(1)}, u32[]{:S(2)}) copy-start(f32[1,128,2048]{1,2,0:T(8,128)S(1)} %copy.103) | copy-start | bytes 3145732
  102.9 76.7 %copy-start.12 = (bf16[384,16,128]{2,1,0:T(8,128)(2,1)S(1)}, bf16[384,16,128]{2,1,0:T(8,128)(2,1)}, u32[]{:S(2)}) copy-start(bf16[384,16,128]{2,1,0:T(8,128)(2,1)} %copy.101) | copy-start | bytes 4718596
  186.3 3.1 copy-start.17
  195.3 9.4 %copy-start = (f32[1,640,16,128]{1,3,2,0:T(8,128)}, f32[1,640,16,128]{1,3,2,0:T(8,128)S(1)}, u32[]{:S(2)}) copy-start(f32[1,640,16,128]{1,3,2,0:T(8,128)S(1)} %get-tuple-element.244) | copy-start | bytes 15728644
  195.8 3.1 copy-start.9
  198.9 354.3 %collective-permute-start.3 = (bf16[2,128,2048]{1,2,0:T(8,128)(2,1)}, bf16[2,128,2048]{1,2,0:T(8,128)(2,1)}, u32[]{:S(2)}, u32[]{:S(2)}) collective-permute-start(bf16[2,128,2048]{1,2,0:T(8,128)(2,1)} %get-tuple-element.234), channel_id=1, source_target_pairs={{1,0},{2,1},{3,2},{4,3},{5,4},{6,5},{7,6},{8,7},{9,8},{10,9},{11,1... | collective-permute-start | bytes 3145736 | tf_op jit(solution)/shard_map/ppermute | solution.py:20
  201.0 352.2 %collective-permute-start.2 = (bf16[2,128,2048]{1,2,0:T(8,128)(2,1)}, bf16[2,128,2048]{1,2,0:T(8,128)(2,1)}, u32[]{:S(2)}, u32[]{:S(2)}) collective-permute-start(bf16[2,128,2048]{1,2,0:T(8,128)(2,1)} %get-tuple-element.233), channel_id=1, source_target_pairs={{0,1},{1,2},{2,3},{3,4},{4,5},{5,6},{6,7},{7,8},{8,9},{9,10},{10,1... | collective-permute-start | bytes 3145736 | tf_op jit(solution)/shard_map/ppermute | solution.py:17
  257.7 279.7 %copy-start.2 = (f32[1,128,2048]{1,2,0:T(8,128)S(1)}, f32[1,128,2048]{1,2,0:T(8,128)}, u32[]{:S(2)}) copy-start(f32[1,128,2048]{1,2,0:T(8,128)} %copy-done.1) | copy-start | bytes 3145732
  257.7 279.7 %copy-start.16 = (bf16[384,16,128]{2,0,1:T(8,128)(2,1)S(1)}, bf16[384,16,128]{2,0,1:T(8,128)(2,1)}, u32[]{:S(2)}) copy-start(bf16[384,16,128]{2,0,1:T(8,128)(2,1)} %copy.105) | copy-start | bytes 4718596
  542.9 10.3 %copy-start.4 = (bf16[1,128,2048]{1,2,0:T(8,128)(2,1)S(1)}, bf16[1,128,2048]{1,2,0:T(8,128)(2,1)}, u32[]{:S(2)}) copy-start(bf16[1,128,2048]{1,2,0:T(8,128)(2,1)} %copy-done.3) | copy-start | bytes 1572868
  542.9 10.3 %copy-start.6 = (bf16[1,128,16,128]{1,3,2,0:T(8,128)(2,1)S(1)}, bf16[1,128,16,128]{1,3,2,0:T(8,128)(2,1)}, u32[]{:S(2)}) copy-start(bf16[1,128,16,128]{1,3,2,0:T(8,128)(2,1)} %copy-done.5) | copy-start | bytes 1572868
  556.6 3.3 copy-start.8
  556.6 3.3 copy-start.10
  559.9 3.8 copy-start.21
  (9 other events, 15.5 us)
Sparse Core Ops, SparseCore 0:
  11.3 82.5 all-gather.4
  97.3 74.6 all-gather.6
  230.5 192.0 all-reduce.5
where the time goes:
time: 656 us; the launch traced here: 654 us
  blocking collectives  362 us (55%)
  waiting for transfers between devices  130 us (20%)
  local copies, waits for them, and re-layouts  60.6 us (9%)
  other arithmetic  58.7 us (9%)
  between operations  15.6 us (2%)
  matrix products  14 us (2%)
  starting transfers between devices  12.9 us (2%)
    unnamed x1, blocking collectives  280 us
    psum x1, blocking collectives, body(): lax.psum((query_gain_vector, key_gain_vector + lyric_gain_vector), ('song...  82.4 us
    all_gather x1, waiting for transfers between devices, body(): lax.all_gather(lyric_norm.reshape(lyric_local, model_width), 'seq', axis=...  69.1 us
    all_gather x1, waiting for transfers between devices, body(): lax.all_gather(lyric_values[0], 'seq', axis=0, tiled=True)  53.5 us
    unnamed x66, local copies, waits for them, and re-layouts  21.5 us
    scatter-add x1, other arithmetic, body(): lyric_grad_val = jnp.zeros((lyric_total, head_count, head_size), jnp.floa...  20.2 us
    scatter-add x1, other arithmetic, body(): lyric_grad_key = jnp.zeros((lyric_total, head_count, head_size), jnp.floa...  20.2 us
  transfers between devices with their start and end apart: 7, of which 4 were waited for; matrix products, arithmetic and copies ran while one was open for 16% of the time, Pallas kernels for 0%

commit v1 on v0

--- a/solution.py
+++ b/solution.py
@@ -191,7 +191,7 @@
         lyric_keys[0], lyric_inv, k_gain, summed_key.reshape(lyric_local, head_count, head_size)
     )
     total_query_gain, total_key_gain = lax.psum(
-        (query_gain_vector, key_gain_vector + lyric_gain_vector), ("song", "seq")
+        lax.psum((query_gain_vector, key_gain_vector + lyric_gain_vector), "song"), "seq"
     )
     return (
         output_list.reshape(1, frames, model_width),

time: 656 us -> 737 us (1.12)
  waiting for transfers between devices: 130 us -> 279 us
  blocking collectives: 362 us -> 290 us
    unnamed x4, waiting for transfers between devices: 0.05 us -> 149 us
    psum x1, blocking collectives: 82.4 us -> 8.46 us  [body(): lax.psum((query_gain_vector, key_gain_vector + lyric_gain_vector), 'song')]
    unnamed x66 -> x78, local copies, waits for them, and re-layouts: 21.5 us -> 22.7 us
  transfers between devices with their start and end apart: 7 -> 7, of which waited for: 4 -> 5; matrix products, arithmetic and copies ran while one was open for 16% -> 12% of each run, Pallas kernels for 0% -> 0%
where the time goes in v1:
time: 737 us; the launch traced here: 732 us
  blocking collectives  290 us (39%)
  waiting for transfers between devices  279 us (38%)
  local copies, waits for them, and re-layouts  62.1 us (8%)
  other arithmetic  56.8 us (8%)
  between operations  15.7 us (2%)
  matrix products  15.3 us (2%)
  starting transfers between devices  12.9 us (2%)
    unnamed x1, blocking collectives  281 us
    unnamed x4, waiting for transfers between devices  149 us
    all_gather x1, waiting for transfers between devices, body(): lax.all_gather(lyric_norm.reshape(lyric_local, model_width), 'seq', axis=...  69.1 us
    all_gather x1, waiting for transfers between devices, body(): lax.all_gather(lyric_values[0], 'seq', axis=0, tiled=True)  53.6 us
    unnamed x78, local copies, waits for them, and re-layouts  22.7 us
    scatter-add x1, other arithmetic, body(): lyric_grad_val = jnp.zeros((lyric_total, head_count, head_size), jnp.floa...  20.2 us
    scatter-add x1, other arithmetic, body(): lyric_grad_key = jnp.zeros((lyric_total, head_count, head_size), jnp.floa...  20.2 us
  transfers between devices with their start and end apart: 7, of which 5 were waited for; matrix products, arithmetic and copies ran while one was open for 12% of the time, Pallas kernels for 0%

profile of v1, /device:TPU:1, one launch (start us, length us, event | category | flops | bytes accessed | tf_op | source)
XLA Modules:
  0.0 732.0 jit_solution(5339710191172339671)
XLA Ops:
  16.1 5.2 collective-permute-start.1
  27.9 5.7 collective-permute-done.1
  40.3 53.6 %all-gather.5.cloned.1.call-done = bf16[1,384,2048]{2,0,1:T(2,128)(2,1)} async-done(((bf16[1,6,2048]{2,0,1:T(2,128)(2,1)}), bf16[1,384,2048]{2,0,1:T(2,128)(2,1)}) %all-gather.5.cloned.1.call-update) | async-done | bytes 1572880 | tf_op jit(solution)/shard_map/all_gather | solution.py:96
  93.9 6.9 copy.100
  102.9 69.1 %all-gather.7.cloned.1.call-done = bf16[64,6,2048]{2,1,0:T(8,128)(2,1)} async-done(((bf16[1,6,2048]{2,1,0:T(8,128)(2,1)}), bf16[64,6,2048]{2,1,0:T(8,128)(2,1)}) %all-gather.7.cloned.1.call-update) | async-done | bytes 1572880 | tf_op jit(solution)/shard_map/all_gather | solution.py:95
  172.0 4.4 reshape.472
  176.4 3.2 gather_fusion.1
  186.3 3.9 fusion.56
  191.0 2.5 multiply_reduce_fusion
  193.4 2.0 copy.114
  195.5 3.8 fusion
  201.0 2.7 fusion.18
  208.7 2.1 collective-permute-start.3
  210.8 3.6 collective-permute-start.2
  216.8 20.2 %scatter_fusion = f32[384,16,128]{2,1,0:T(8,128)S(1)} fusion(f32[384,16,128]{2,1,0:T(8,128)S(1)} %broadcast.403.clone, s32[256]{0:T(256)S(1)} %bitcast.227, f32[256,16,128]{2,1,0:T(8,128)} %copy.112), kind=kCustom, calls=%fused_computation.2 | custom fusion | flops 524288 | bytes 6292480 | tf_op jit(solution)/shard_map/scatter-add | solution.py:134
  237.1 3.0 copy.146
  243.0 2.4 slice.228
  249.3 20.2 %scatter_fusion.1 = f32[384,16,128]{2,1,0:T(8,128)S(1)} fusion(f32[384,16,128]{2,1,0:T(8,128)S(1)} %broadcast.403.clone.1, s32[256]{0:T(256)S(1)} %bitcast.228, f32[256,16,128]{2,1,0:T(8,128)} %copy.113), kind=kCustom, calls=%fused_computation.3 | custom fusion | flops 524288 | bytes 6292480 | tf_op jit(solution)/shard_map/scatter-add | solution.py:139
  269.6 3.1 copy.145
  277.7 2.7 fusion.16
  280.4 2.0 copy.117
  282.5 148.9 %all-reduce.7.cloned.1.call-done = f32[384,2048]{1,0:T(8,128)} async-done(((f32[384,2048]{1,0:T(8,128)}), f32[384,2048]{1,0:T(8,128)}) %all-reduce.7.cloned.1.call-update) | async-done | bytes 3145744
  434.1 8.5 %all-reduce.3 = (f32[128]{0:T(128)S(1)}, f32[128]{0:T(128)S(1)}) all-reduce(f32[128]{0:T(128)S(1)} %get-tuple-element.214, f32[128]{0:T(128)S(1)} %add.206), channel_id=1, replica_groups=mesh['song'=4,'seq'=64] {'song'}, use_global_device_ids=true, to_apply=%region_13.15 | all-reduce | flops 256 | bytes 2048 | tf_op jit(solution)/shard_map/psum | solution.py:194
  442.5 281.4 %all-reduce.8 = (bf16[384,2048]{1,0:T(8,128)(2,1)}, f32[128]{0:T(128)}, f32[128]{0:T(128)}) all-reduce(f32[384,2048]{1,0:T(8,128)S(1)} %bitcast.202, f32[128]{0:T(128)S(1)} %get-tuple-element.219, f32[128]{0:T(128)S(1)} %get-tuple-element.220), channel_id=4, replica_groups=mesh['song'=4,'seq'=64] {'seq'}, use_global_device_ids=true, to_apply=%region_11.13.clone | all-reduce | flops 786688 | bytes 4720640
  (138 shorter events, 55.2 us)
Async XLA Ops:
  7.2 86.8 %all-gather.5.cloned.1.call-start = ((), (), s32[]{:S(2)}) async-start(), calls=%async_computation | async-start | bytes 3194880 | tf_op jit(solution)/shard_map/all_gather | solution.py:96
  8.7 163.3 %all-gather.7.cloned.1.call-start = ((), (), s32[]{:S(2)}) async-start(), calls=%async_computation.1 | async-start | bytes 2129920 | tf_op jit(solution)/shard_map/all_gather | solution.py:95
  11.7 419.6 %all-reduce.7.cloned.1.call-start = ((), (), s32[]{:S(2)}) async-start(), calls=%async_computation.2 | async-start | bytes 6291456
  13.1 10.8 %copy-start.29 = (s32[1,1,2]{2,1,0:T(1,128)S(1)}, s32[1,1,2]{2,1,0:T(1,128)}, u32[]{:S(2)}) copy-start(s32[1,1,2]{2,1,0:T(1,128)} %param.44) | copy-start | bytes 28
  13.1 10.9 %copy-start.24 = (bf16[1,128,2048]{2,1,0:T(8,128)(2,1)S(1)}, bf16[1,128,2048]{2,1,0:T(8,128)(2,1)}, u32[]{:S(2)}) copy-start(bf16[1,128,2048]{2,1,0:T(8,128)(2,1)} %param.43) | copy-start | bytes 1572868
  14.5 9.5 %copy-start.3 = (bf16[1,128,2048]{1,2,0:T(8,128)(2,1)}, bf16[1,128,2048]{1,2,0:T(8,128)(2,1)S(1)}, u32[]{:S(2)}) copy-start(bf16[1,128,2048]{1,2,0:T(8,128)(2,1)S(1)} %copy.97) | copy-start | bytes 1572868
  15.6 10.7 %copy-start.30 = (u32[256]{0:T(256)S(1)}, u32[256]{0:T(256)}, u32[]{:S(2)}) copy-start(u32[256]{0:T(256)} %constant.274) | copy-start | bytes 3076
  16.0 11.7 %copy-start.28 = (f32[128]{0:T(128)S(1)}, f32[128]{0:T(128)}, u32[]{:S(2)}) copy-start(f32[128]{0:T(128)} %param.41) | copy-start | bytes 1540
  16.1 17.4 %collective-permute-start.1 = (bf16[2,128,2048]{1,2,0:T(8,128)(2,1)S(1)}, bf16[2,128,2048]{1,2,0:T(8,128)(2,1)}, u32[]{:S(2)}, u32[]{:S(2)}) collective-permute-start(bf16[2,128,2048]{1,2,0:T(8,128)(2,1)S(1)} %pad_maximum_fusion.9), channel_id=1, source_target_pairs={{1,0},{2,1},{3,2},{4,3},{5,4},{6,5},{7,6},{8,7},{9,8},{10,9},{11,1... | collective-permute-start | bytes 3145736 | tf_op jit(solution)/shard_map/ppermute | solution.py:20
  21.3 14.2 %collective-permute-start = (bf16[2,128,2048]{1,2,0:T(8,128)(2,1)S(1)}, bf16[2,128,2048]{1,2,0:T(8,128)(2,1)}, u32[]{:S(2)}, u32[]{:S(2)}) collective-permute-start(bf16[2,128,2048]{1,2,0:T(8,128)(2,1)S(1)} %pad_maximum_fusion.9), channel_id=1, source_target_pairs={{0,1},{1,2},{2,3},{3,4},{4,5},{5,6},{6,7},{7,8},{8,9},{9,10},{10,1... | collective-permute-start | bytes 3145736 | tf_op jit(solution)/shard_map/ppermute | solution.py:17
  26.3 173.9 %copy-start.1 = (f32[1,128,2048]{1,2,0:T(8,128)}, f32[1,128,2048]{1,2,0:T(8,128)S(1)}, u32[]{:S(2)}) copy-start(f32[1,128,2048]{1,2,0:T(8,128)S(1)} %copy.103) | copy-start | bytes 3145732
  102.9 76.6 %copy-start.15 = (bf16[384,16,128]{2,1,0:T(8,128)(2,1)S(1)}, bf16[384,16,128]{2,1,0:T(8,128)(2,1)}, u32[]{:S(2)}) copy-start(bf16[384,16,128]{2,1,0:T(8,128)(2,1)} %copy.101) | copy-start | bytes 4718596
  184.7 5.5 copy-start.22
  186.3 4.7 copy-start.31
  186.3 4.7 copy-start.19
  201.0 13.5 %copy-start = (f32[1,640,16,128]{1,3,2,0:T(8,128)}, f32[1,640,16,128]{1,3,2,0:T(8,128)S(1)}, u32[]{:S(2)}) copy-start(f32[1,640,16,128]{1,3,2,0:T(8,128)S(1)} %get-tuple-element.247) | copy-start | bytes 15728644
  208.7 64.1 %collective-permute-start.3 = (bf16[2,128,2048]{1,2,0:T(8,128)(2,1)}, bf16[2,128,2048]{1,2,0:T(8,128)(2,1)}, u32[]{:S(2)}, u32[]{:S(2)}) collective-permute-start(bf16[2,128,2048]{1,2,0:T(8,128)(2,1)} %get-tuple-element.237), channel_id=1, source_target_pairs={{1,0},{2,1},{3,2},{4,3},{5,4},{6,5},{7,6},{8,7},{9,8},{10,9},{11,1... | collective-permute-start | bytes 3145736 | tf_op jit(solution)/shard_map/ppermute | solution.py:20
  210.8 62.0 %collective-permute-start.2 = (bf16[2,128,2048]{1,2,0:T(8,128)(2,1)}, bf16[2,128,2048]{1,2,0:T(8,128)(2,1)}, u32[]{:S(2)}, u32[]{:S(2)}) collective-permute-start(bf16[2,128,2048]{1,2,0:T(8,128)(2,1)} %get-tuple-element.236), channel_id=1, source_target_pairs={{0,1},{1,2},{2,3},{3,4},{4,5},{5,6},{6,7},{7,8},{8,9},{9,10},{10,1... | collective-permute-start | bytes 3145736 | tf_op jit(solution)/shard_map/ppermute | solution.py:17
  269.6 3.2 copy-start.4
  269.6 3.2 copy-start.6
  269.6 3.2 copy-start.8
  269.6 3.2 copy-start.10
  277.7 154.7 %copy-start.26 = (bf16[1,6,2048]{2,1,0:T(8,128)(2,1)S(1)}, bf16[1,6,2048]{2,1,0:T(8,128)(2,1)}, u32[]{:S(2)}) copy-start(bf16[1,6,2048]{2,1,0:T(8,128)(2,1)} %param.39) | copy-start | bytes 73732
  277.7 164.8 %copy-start.5 = (f32[48,8,16,128]{3,1,2,0:T(8,128)S(1)}, f32[48,8,16,128]{3,1,2,0:T(8,128)}, u32[]{:S(2)}) copy-start(f32[48,8,16,128]{3,1,2,0:T(8,128)} %copy.145) | copy-start | bytes 9437188
  (15 other events, 27.7 us)
Sparse Core Ops, SparseCore 0:
  11.3 82.5 all-gather.4
  97.3 74.6 all-gather.6
  240.2 191.0 all-reduce.6
